TPU v7x, 32 devices: a whole 2x2x4 slice. The times are simulated.
32 devices in a mesh: pole: 2 (over x), prow: 8 (over z, y), pcol: 2 (over core).
Axes of the slice: x: 2, y: 2, z: 4, core: 2. Of those that a mesh axis runs over, the one named last changes fastest.
Arguments:
- ancestor_inverse: bfloat16 [8192, 4096], P(('pole', 'prow'), 'pcol'), parts along dimension 0, may hold values from -6 to 6
- l_panel: bfloat16 [8192, 1024], P(('pole', 'prow'), 'pcol'), parts along dimension 0, may hold values from -0.125 to 0.125
- diag_inverse: float32 [2048, 256], P(('pole', 'pcol')), parts along dimension 0, may hold values from -6 to 6
- pattern: int32 [4, 8], replicated, may hold values from 0 to 15, as said below
Outputs:
- column_blocks: float32 [8192, 1024], P(('pole', 'prow'), 'pcol'), parts along dimension 0
- diag_blocks: float32 [2048, 256], P(('pole', 'pcol')), parts along dimension 0
There are 2 independent parts, one for each index of `pole`. A program takes and returns all parts, laid end to end along the dimension named above; an argument that names none is the same for every part. Nothing has to cross between parts.
Inputs may be any that keep to these rules, and one draw needn't show every extreme that they name: `pattern`: each row lists 8 different ancestor supernodes in increasing order, and every row lists ancestor 16 - 1.
All inputs are finite; a program needn't handle non-finite values.
Results may differ from a plain program's by a relative error of at most 0.0003.
Values may be sent and summed in bfloat16 or wider, within the bound.
No kernel may reach another device: no remote copies, remote signals or barrier semaphores. Data moves between devices by JAX's collectives and lax.ppermute only.
A program may use at most 128 MiB of HBM per device.

v0:
```python
import jax
import jax.numpy as jnp
from jax import lax
from jax.sharding import PartitionSpec as P

B = 256


def per_device(ancestor_inverse, l_panel, diag_inverse, pattern):
    row_index = lax.axis_index("prow")
    col_index = lax.axis_index("pcol")
    local_tiles = l_panel.shape[0] // B
    local_nodes = l_panel.shape[1] // B
    tile_ids = row_index * local_tiles + jnp.arange(local_tiles, dtype=jnp.int32)
    node_rows = lax.dynamic_slice_in_dim(pattern, col_index * local_nodes, local_nodes, 0)
    member = jnp.any(node_rows[None, :, :] == tile_ids[:, None, None], axis=2)
    panel_mask = member.astype(jnp.float32)[:, None, :, None]
    masked = (
        l_panel.reshape(local_tiles, B, local_nodes, B) * panel_mask.astype(jnp.bfloat16)
    ).reshape(l_panel.shape)
    swapped = lax.all_to_all(masked, "pcol", split_axis=0, concat_axis=1, tiled=True)
    partial_sum = jnp.dot(
        ancestor_inverse,
        lax.all_gather(swapped, "prow", axis=0, tiled=True),
        preferred_element_type=jnp.float32,
    )
    summed = lax.psum_scatter(partial_sum, "pcol", scatter_dimension=1, tiled=True)
    negated = -summed
    diag_terms = jnp.einsum(
        "rkb,rkc->kbc",
        masked.astype(jnp.float32).reshape(-1, local_nodes, B),
        negated.reshape(-1, local_nodes, B),
        precision=lax.Precision.HIGHEST,
    )
    totals = lax.psum(diag_terms, "prow")
    diag_blocks = diag_inverse - totals.reshape(local_nodes * B, B)
    column_blocks = (negated.reshape(local_tiles, B, local_nodes, B) * panel_mask).reshape(
        negated.shape
    )
    return (column_blocks, diag_blocks)


def solution(mesh):
    return jax.shard_map(
        per_device,
        mesh=mesh,
        in_specs=(
            P(("pole", "prow"), "pcol"),
            P(("pole", "prow"), "pcol"),
            P(("pole", "pcol"), None),
            P(),
        ),
        out_specs=(P(("pole", "prow"), "pcol"), P(("pole", "pcol"), None)),
        check_vma=False,
    )
```

profile of v0, /device:TPU:0, one launch (start us, length us, event | category | flops | bytes accessed | tf_op | source)
XLA Modules:
  0.0 193.1 jit_solution(15879236275212393171)
XLA Ops:
  7.2 0.8 constant_dynamic-slice_fusion
  8.1 0.2 compare_reduce_fusion
  8.3 0.3 mul.39
  8.6 0.1 copy.27
  8.7 1.2 mul.41
  9.9 4.2 %all_to_all.19 = bf16[2,256,512]{2,1,0:T(8,128)(2,1)S(1)} all-to-all(bf16[2,256,512]{2,1,0:T(8,128)(2,1)S(1)} %bitcast.30), channel_id=1, replica_groups=mesh['pole'=2,'prow'=8,'pcol'=2] {'pcol'}, dimensions={0} | all-to-all | bytes 1048576 | tf_op jit(solution)/shard_map/all_to_all | solution.py:21
  14.1 1.0 copy.19
  15.1 0.0 reduce-scatter.2.cloned.1.call-start
  15.1 77.5 %all-gather.2.cloned.1.call-done = bf16[2048,1024]{0,1:T(8,128)(2,1)} async-done(((bf16[256,1024]{0,1:T(8,128)(2,1)}), bf16[2048,1024]{0,1:T(8,128)(2,1)}) %all-gather.2.cloned.1.call-update) | async-done | bytes 4194320 | tf_op jit(solution)/shard_map/all_gather | solution.py:24
  92.6 5.9 %convolution_bitcast_fusion = f32[512,1024]{0,1:T(8,128)} fusion(bf16[2048,1024]{0,1:T(8,128)(2,1)} %all-gather.2.cloned.1.call-done, bf16[512,2048]{1,0:T(8,128)(2,1)S(1)} %copy-done), kind=kOutput, calls=%fused_computation | convolution fusion | flops 2147483648 | bytes 8388608 | tf_op jit(solution)/shard_map/dot_general | solution.py:22
  98.5 0.0 all-reduce.2.cloned.1.call-start
  98.6 0.1 copy.21
  98.7 0.9 copy-done.1
  99.5 1.0 copy.26
  100.5 0.1 copy.20
  100.6 0.3 mul.42
  101.0 1.0 copy.28
  102.0 0.1 broadcast_bitcast_fusion
  102.1 4.5 %reduce-scatter.2.cloned.1.call-done = f32[512,512]{0,1:T(8,128)} async-done(((f32[512,1024]{0,1:T(8,128)}), f32[512,512]{0,1:T(8,128)}) %reduce-scatter.2.cloned.1.call-update) | async-done | bytes 1048592 | tf_op jit(solution)/shard_map/reduce_scatter | solution.py:27
  106.6 1.8 fusion.3
  108.5 1.5 fusion
  110.0 1.3 copy.24
  111.3 73.3 %all-reduce.2.cloned.1.call-done = f32[512,256]{1,0:T(8,128)} async-done(((f32[512,256]{1,0:T(8,128)}), f32[512,256]{1,0:T(8,128)}) %all-reduce.2.cloned.1.call-update) | async-done | bytes 524304 | tf_op jit(solution)/shard_map/psum | solution.py:35
  184.6 2.1 %sub.3 = f32[512,256]{1,0:T(8,128)} subtract(f32[512,256]{1,0:T(8,128)} %param.6, f32[512,256]{1,0:T(8,128)} %all-reduce.2.cloned.1.call-done) | non-fusion elementwise | flops 131072 | bytes 1572864 | tf_op jit(solution)/shard_map/sub | solution.py:36
  (12 shorter events, 0.1 us)
Async XLA Ops:
  7.2 85.5 %copy-start = (bf16[512,2048]{1,0:T(8,128)(2,1)S(1)}, bf16[512,2048]{1,0:T(8,128)(2,1)}, u32[]{:S(2)}) copy-start(bf16[512,2048]{1,0:T(8,128)(2,1)} %param.4) | copy-start | bytes 6291460
  7.2 85.4 %all-gather.2.cloned.1.call-start = ((), (), s32[]{:S(2)}) async-start(), calls=%async_computation.2 | async-start | bytes 4718592 | tf_op jit(solution)/shard_map/all_gather | solution.py:24
  15.1 91.5 %reduce-scatter.2.cloned.1.call-start = ((), (), s32[]{:S(2)}) async-start(), calls=%async_computation.3 | async-start | bytes 3145728 | tf_op jit(solution)/shard_map/reduce_scatter | solution.py:27
  98.5 1.0 copy-start.1
  98.5 86.0 %all-reduce.2.cloned.1.call-start = ((), (), s32[]{:S(2)}) async-start(), calls=%async_computation.4 | async-start | bytes 1048576 | tf_op jit(solution)/shard_map/psum | solution.py:35
  106.6 1.8 copy-start.2
Sparse Core Ops, SparseCore 0:
  15.2 77.3 all-gather.1
  98.6 7.9 reduce-scatter.1
  110.6 73.9 all-reduce.1
where the time goes:
time: 193 us
  waiting for transfers between devices  155 us (80%)
  between operations  13.8 us (7%)
  matrix products  7.35 us (4%)
  local copies, waits for them, and re-layouts  7.1 us (4%)
  other arithmetic  5.29 us (3%)
  blocking collectives  4.15 us (2%)
    all_gather x1, waiting for transfers between devices, per_device(): lax.all_gather(swapped, 'prow', axis=0, tiled=True)  77.5 us
    psum x1, waiting for transfers between devices, per_device(): totals = lax.psum(diag_terms, 'prow')  73.3 us
    dot_general x1, matrix products, per_device(): jnp.dot(ancestor_inverse, lax.all_gather(swapped, 'prow', axis=0, tiled=T...  5.87 us
    reduce_scatter x1, waiting for transfers between devices, per_device(): lax.psum_scatter(partial_sum, 'pcol', scatter_dimension=1, tiled=True)  4.52 us
    all_to_all x1, blocking collectives, per_device(): lax.all_to_all(masked, 'pcol', split_axis=0, concat_axis=1, tiled=True)  4.15 us
  transfers between devices with their start and end apart: 3, of which 3 were waited for; matrix products, arithmetic and copies ran while one was open for 2% of the time, Pallas kernels for 0%

commit v1 on v0

--- a/solution.py
+++ b/solution.py
@@ -1,9 +1,21 @@
+import functools
 import jax
 import jax.numpy as jnp
 from jax import lax
 from jax.sharding import PartitionSpec as P
 
 B = 256
+
+
+def raise_signs(array_in, comm_axis):
+    v1 = array_in
+    world = lax.axis_size(comm_axis)
+    for i0 in [num for num in (1, 2, 4, 8, 16) if num < world]:
+        v1 = v1 + lax.ppermute(v1, comm_axis, [(ix, ix ^ i0) for ix in range(world)])
+    return v1
+
+
+_search_set = functools.partial(raise_signs, comm_axis="prow")
 
 
 def per_device(ancestor_inverse, l_panel, diag_inverse, pattern):
@@ -32,7 +44,7 @@
         negated.reshape(-1, local_nodes, B),
         precision=lax.Precision.HIGHEST,
     )
-    totals = lax.psum(diag_terms, "prow")
+    totals = _search_set(diag_terms)
     diag_blocks = diag_inverse - totals.reshape(local_nodes * B, B)
     column_blocks = (negated.reshape(local_tiles, B, local_nodes, B) * panel_mask).reshape(
         negated.shape

time: 193 us -> 173 us (0.90)
  waiting for transfers between devices: 155 us -> 127 us
  starting transfers between devices: 0.12 us -> 6.24 us
  other arithmetic: 5.29 us -> 7.31 us
    psum x1 -> x0, waiting for transfers between devices: 73.3 us -> none  [per_device(): totals = lax.psum(diag_terms, 'prow')]
    ppermute x0 -> x3, waiting for transfers between devices: none -> 45 us  [raise_signs(): lax.ppermute(v1, comm_axis, [(ix, ix ^ i0) for ix in range(world)])]
    ppermute x0 -> x3, starting transfers between devices: none -> 6.16 us  [raise_signs(): lax.ppermute(v1, comm_axis, [(ix, ix ^ i0) for ix in range(world)])]
    add x0 -> x3, other arithmetic: none -> 2.2 us  [raise_signs(): v1 + lax.ppermute(v1, comm_axis, [(ix, ix ^ i0) for ix in range(world)])]
  transfers between devices with their start and end apart: 3 -> 5, of which waited for: 3 -> 5; matrix products, arithmetic and copies ran while one was open for 2% -> 2% of each run, Pallas kernels for 0% -> 0%
where the time goes in v1:
time: 173 us
  waiting for transfers between devices  127 us (73%)
  between operations  14.1 us (8%)
  other arithmetic  7.31 us (4%)
  local copies, waits for them, and re-layouts  7.15 us (4%)
  matrix products  6.56 us (4%)
  starting transfers between devices  6.24 us (4%)
  blocking collectives  4.15 us (2%)
    all_gather x1, waiting for transfers between devices, per_device(): lax.all_gather(swapped, 'prow', axis=0, tiled=True)  77.5 us
    ppermute x3, waiting for transfers between devices, raise_signs(): lax.ppermute(v1, comm_axis, [(ix, ix ^ i0) for ix in range(world)])  45 us
    ppermute x3, starting transfers between devices, raise_signs(): lax.ppermute(v1, comm_axis, [(ix, ix ^ i0) for ix in range(world)])  6.16 us
    dot_general x1, matrix products, per_device(): jnp.dot(ancestor_inverse, lax.all_gather(swapped, 'prow', axis=0, tiled=T...  5.87 us
    reduce_scatter x1, waiting for transfers between devices, per_device(): lax.psum_scatter(partial_sum, 'pcol', scatter_dimension=1, tiled=True)  4.52 us
    all_to_all x1, blocking collectives, per_device(): lax.all_to_all(masked, 'pcol', split_axis=0, concat_axis=1, tiled=True)  4.15 us
  transfers between devices with their start and end apart: 5, of which 5 were waited for; matrix products, arithmetic and copies ran while one was open for 2% of the time, Pallas kernels for 0%

profile of v1, /device:TPU:0, one launch (start us, length us, event | category | flops | bytes accessed | tf_op | source)
XLA Modules:
  0.0 172.6 jit_solution(1449604601416536138)
XLA Ops:
  7.2 0.8 constant_dynamic-slice_fusion
  8.3 0.3 mul.39
  8.7 1.2 mul.41
  9.9 4.2 %all_to_all.19 = bf16[2,256,512]{2,1,0:T(8,128)(2,1)S(1)} all-to-all(bf16[2,256,512]{2,1,0:T(8,128)(2,1)S(1)} %bitcast.30), channel_id=1, replica_groups=mesh['pole'=2,'prow'=8,'pcol'=2] {'pcol'}, dimensions={0} | all-to-all | bytes 1048576 | tf_op jit(solution)/shard_map/all_to_all | solution.py:33
  14.1 1.0 copy.19
  15.1 77.5 %all-gather.2.cloned.1.call-done = bf16[2048,1024]{0,1:T(8,128)(2,1)} async-done(((bf16[256,1024]{0,1:T(8,128)(2,1)}), bf16[2048,1024]{0,1:T(8,128)(2,1)}) %all-gather.2.cloned.1.call-update) | async-done | bytes 4194320 | tf_op jit(solution)/shard_map/all_gather | solution.py:36
  92.6 5.9 %convolution_bitcast_fusion = f32[512,1024]{0,1:T(8,128)} fusion(bf16[2048,1024]{0,1:T(8,128)(2,1)} %all-gather.2.cloned.1.call-done, bf16[512,2048]{1,0:T(8,128)(2,1)S(1)} %copy-done), kind=kOutput, calls=%fused_computation | convolution fusion | flops 2147483648 | bytes 8388608 | tf_op jit(solution)/shard_map/dot_general | solution.py:34
  98.6 0.9 copy-done.1
  99.5 1.0 copy.26
  100.6 0.3 mul.42
  101.0 1.0 copy.28
  102.1 4.5 %reduce-scatter.2.cloned.1.call-done = f32[512,512]{0,1:T(8,128)} async-done(((f32[512,1024]{0,1:T(8,128)}), f32[512,512]{0,1:T(8,128)}) %reduce-scatter.2.cloned.1.call-update) | async-done | bytes 1048592 | tf_op jit(solution)/shard_map/reduce_scatter | solution.py:39
  106.6 1.8 %fusion.3 = (f32[512,512]{0,1:T(8,128)S(1)}, f32[512,512]{0,1:T(8,128)S(1)}) fusion(f32[512,512]{0,1:T(8,128)} %reduce-scatter.2.cloned.1.call-done, f32[512,512]{0,1:T(8,128)} %bitcast.27), kind=kLoop, calls=%fused_computation.11 | loop fusion | flops 524288 | bytes 4194304 | tf_op jit(solution)/shard_map/neg | solution.py:40
  108.5 0.7 fusion
  109.2 2.0 %collective-permute-start = (f32[2,256,256]{2,1,0:T(8,128)S(1)}, f32[2,256,256]{2,1,0:T(8,128)S(1)}, u32[]{:S(2)}, u32[]{:S(2)}) collective-permute-start(f32[2,256,256]{2,1,0:T(8,128)S(1)} %fusion), channel_id=1, source_target_pairs={{0,2},{2,0},{4,6},{6,4},{8,10},{10,8},{12,14},{14,12},{1,3},{3,1},... | collective-permute-start | bytes 1572872 | tf_op jit(solution)/shard_map/ppermute | solution.py:14
  111.1 12.3 %collective-permute-done = f32[2,256,256]{2,1,0:T(8,128)S(1)} collective-permute-done((f32[2,256,256]{2,1,0:T(8,128)S(1)}, f32[2,256,256]{2,1,0:T(8,128)S(1)}, u32[]{:S(2)}, u32[]{:S(2)}) %collective-permute-start) | collective-permute-done | bytes 524320 | tf_op jit(solution)/shard_map/ppermute | solution.py:14
  123.5 1.7 %collective-permute-start.1 = (f32[2,256,256]{2,1,0:T(8,128)S(1)}, f32[2,256,256]{2,1,0:T(8,128)S(1)}, u32[]{:S(2)}, u32[]{:S(2)}) collective-permute-start(f32[2,256,256]{2,1,0:T(8,128)S(1)} %add.27), channel_id=1, source_target_pairs={{0,4},{2,6},{4,0},{6,2},{8,12},{10,14},{12,8},{14,10},{1,5},{3,7},... | collective-permute-start | bytes 1572872 | tf_op jit(solution)/shard_map/ppermute | solution.py:14
  125.2 11.6 %collective-permute-done.1 = f32[2,256,256]{2,1,0:T(8,128)S(1)} collective-permute-done((f32[2,256,256]{2,1,0:T(8,128)S(1)}, f32[2,256,256]{2,1,0:T(8,128)S(1)}, u32[]{:S(2)}, u32[]{:S(2)}) %collective-permute-start.1) | collective-permute-done | bytes 524320 | tf_op jit(solution)/shard_map/ppermute | solution.py:14
  136.8 0.9 add.28
  137.7 2.5 %collective-permute-start.2 = (f32[2,256,256]{2,1,0:T(8,128)}, f32[2,256,256]{2,1,0:T(8,128)}, u32[]{:S(2)}, u32[]{:S(2)}) collective-permute-start(f32[2,256,256]{2,1,0:T(8,128)} %add.28), channel_id=1, source_target_pairs={{0,8},{2,10},{4,12},{6,14},{8,0},{10,2},{12,4},{14,6},{1,9},{3,11}... | collective-permute-start | bytes 1572872 | tf_op jit(solution)/shard_map/ppermute | solution.py:14
  140.1 1.3 copy.24
  141.4 21.1 %collective-permute-done.2 = f32[2,256,256]{2,1,0:T(8,128)} collective-permute-done((f32[2,256,256]{2,1,0:T(8,128)}, f32[2,256,256]{2,1,0:T(8,128)}, u32[]{:S(2)}, u32[]{:S(2)}) %collective-permute-start.2) | collective-permute-done | bytes 524320 | tf_op jit(solution)/shard_map/ppermute | solution.py:14
  162.6 1.3 add.29
  163.8 1.9 %bitcast_subtract_fusion = f32[512,256]{1,0:T(8,128)} fusion(f32[512,256]{1,0:T(8,128)} %param.6, f32[2,256,256]{2,1,0:T(8,128)S(1)} %add.29), kind=kLoop, calls=%fused_computation.1 | loop fusion | flops 131072 | bytes 1572864 | tf_op jit(solution)/shard_map/sub | solution.py:48
  (18 shorter events, 0.8 us)
Async XLA Ops:
  7.2 85.5 %copy-start = (bf16[512,2048]{1,0:T(8,128)(2,1)S(1)}, bf16[512,2048]{1,0:T(8,128)(2,1)}, u32[]{:S(2)}) copy-start(bf16[512,2048]{1,0:T(8,128)(2,1)} %param.4) | copy-start | bytes 6291460
  7.2 85.4 %all-gather.2.cloned.1.call-start = ((), (), s32[]{:S(2)}) async-start(), calls=%async_computation.2 | async-start | bytes 4718592 | tf_op jit(solution)/shard_map/all_gather | solution.py:36
  15.1 91.5 %reduce-scatter.2.cloned.1.call-start = ((), (), s32[]{:S(2)}) async-start(), calls=%async_computation.3 | async-start | bytes 3145728 | tf_op jit(solution)/shard_map/reduce_scatter | solution.py:39
  98.5 1.0 copy-start.1
  106.6 1.8 %copy-start.2 = (bf16[512,512]{0,1:T(8,128)(2,1)S(1)}, bf16[512,512]{0,1:T(8,128)(2,1)}, u32[]{:S(2)}) copy-start(bf16[512,512]{0,1:T(8,128)(2,1)} %copy.26) | copy-start | bytes 1572868
  109.2 14.2 %collective-permute-start = (f32[2,256,256]{2,1,0:T(8,128)S(1)}, f32[2,256,256]{2,1,0:T(8,128)S(1)}, u32[]{:S(2)}, u32[]{:S(2)}) collective-permute-start(f32[2,256,256]{2,1,0:T(8,128)S(1)} %fusion), channel_id=1, source_target_pairs={{0,2},{2,0},{4,6},{6,4},{8,10},{10,8},{12,14},{14,12},{1,3},{3,1},... | collective-permute-start | bytes 1572872 | tf_op jit(solution)/shard_map/ppermute | solution.py:14
  123.5 13.4 %collective-permute-start.1 = (f32[2,256,256]{2,1,0:T(8,128)S(1)}, f32[2,256,256]{2,1,0:T(8,128)S(1)}, u32[]{:S(2)}, u32[]{:S(2)}) collective-permute-start(f32[2,256,256]{2,1,0:T(8,128)S(1)} %add.27), channel_id=1, source_target_pairs={{0,4},{2,6},{4,0},{6,2},{8,12},{10,14},{12,8},{14,10},{1,5},{3,7},... | collective-permute-start | bytes 1572872 | tf_op jit(solution)/shard_map/ppermute | solution.py:14
  137.7 24.9 %collective-permute-start.2 = (f32[2,256,256]{2,1,0:T(8,128)}, f32[2,256,256]{2,1,0:T(8,128)}, u32[]{:S(2)}, u32[]{:S(2)}) collective-permute-start(f32[2,256,256]{2,1,0:T(8,128)} %add.28), channel_id=1, source_target_pairs={{0,8},{2,10},{4,12},{6,14},{8,0},{10,2},{12,4},{14,6},{1,9},{3,11}... | collective-permute-start | bytes 1572872 | tf_op jit(solution)/shard_map/ppermute | solution.py:14
Sparse Core Ops, SparseCore 0:
  15.2 77.3 all-gather.1
  98.6 7.9 reduce-scatter.1
